TPU v7x, 512 devices: a whole 4x8x8 slice. The times are simulated.
512 devices in a mesh: row: 32 (over x_hi, y, core), col: 16 (over z, x_lo).
Axes of the slice: x: 4 (x_hi: 2, x_lo: 2; x = x_hi * 2 + x_lo), y: 8, z: 8, core: 2. Of those that a mesh axis runs over, the one named last changes fastest.
Arguments:
- schur_tile: float32 [8192, 8192], P('row', 'col'), may hold values from -2 to 6, as said below
- swap_mask: int32 [2, 32], P(None, 'row'), may hold values from 0 to 1, as said below
Outputs:
- reordered: float32 [8192, 8192], P('row', 'col')
Inputs may be any that keep to these rules, and one draw needn't show every extreme that they name: schur_tile is upper triangular; the diagonal entries of rows j * 128 to j * 128 + 127 lie within 0.15 of 0.75 + 1.5 (j mod 4). swap_mask[1, 31] is 0.
All inputs are finite; a program needn't handle non-finite values.
Results may differ from a plain program's by a relative error of at most 0.0003.
Values sent between devices are 32-bit elements; how exact they have to be, the bound alone decides.
No kernel may reach another device: no remote copies, remote signals or barrier semaphores. Data moves between devices by JAX's collectives and lax.ppermute only.
A program may use at most 64 MiB of HBM per device.

v0:
```python
import jax
import jax.numpy as jnp
from jax import lax
from jax.experimental import pallas as pl
from jax.experimental.pallas import tpu as pltpu
from jax.sharding import PartitionSpec as P

K = 128


AXES = ("row", "col")


NN=((1,),(0,)); NT=((1,),(1,))


def halves(x):
    hi = x.astype(jnp.bfloat16)
    return hi, (x - hi.astype(jnp.float32)).astype(jnp.bfloat16)


def dot1(a, b, dims):
    return lax.dot_general(a, b, (dims, ((), ())), preferred_element_type=jnp.float32)


def mm(a, b, dims=NN):
    ah, al = halves(a); bh, bl = halves(b)
    return dot1(ah, bh, dims) + (dot1(ah, bl, dims) + dot1(al, bh, dims))


def mlow(a, b, dims=NN):
    return dot1(a.astype(jnp.bfloat16), b.astype(jnp.bfloat16), dims)


def grids():
    i = lax.broadcasted_iota(jnp.int32, (K, K), 0)
    j = lax.broadcasted_iota(jnp.int32, (K, K), 1)
    return (i == j).astype(jnp.float32), jnp.where(i > j, 1.0, jnp.where(i == j, 0.5, 0.0))


def worst(parts):
    sums = [jnp.sum(x * x) for x in parts]
    top = sums[0]
    for value in sums[1:]:
        top = jnp.where(value <= top, top, value)
    return top


def fast_inverse_cholesky(s_list, eye, phi):
    ws = []
    for s in s_list:
        d = s * eye
        dr = lax.rsqrt(jnp.sum(d, axis=0, keepdims=True)); dc = lax.rsqrt(jnp.sum(d, axis=1, keepdims=True))
        ws.append((s * dc * dr - eye, dr))
    ps = [phi * e for e, _ in ws]
    qs = [mlow(p, p, NT) for p in ps]
    ps = [phi * (e - q) for (e, _), q in zip(ws, qs)]
    qs = [mlow(p, p) for p in ps]
    w = [(eye - p + q) * dr for p, q, (_, dr) in zip(ps, qs, ws)]
    for last in range(2):
        dot = mm if last else mlow
        t = [dot(a, s) for a, s in zip(w, s_list)]
        e = [dot(a, b, NT) - eye for a, b in zip(t, w)]
        u = [dot(phi * b, a) for a, b in zip(w, e)]
        w = [a - b for a, b in zip(w, u)]
    return w, worst(e)


def fast_inverse(a_list, eye):
    cs = [K / jnp.sum(a * eye) for a in a_list]
    r = [eye - a * c for a, c in zip(a_list, cs)]
    r2 = [mm(x, x) for x in r]
    pa = [eye + x for x in r]
    r4 = [mm(x, x) for x in r2]
    pa = [p + mm(q, p) for p, q in zip(pa, r2)]
    return [(p + mm(q, p)) * c for p, q, c in zip(pa, r4, cs)], worst(r4)


def finish(m, c, nop):
    x = [mm(a, b) for a, b in zip(m, c)]
    t = [mm(a, b) for a, b in zip(x, nop)]
    m2 = [mm(a, a) for a in m]
    n2 = [mm(a, a) for a in nop]
    x = [a + mm(b, q) for a, b, q in zip(x, m, t)]
    t = [mm(a, b) for a, b in zip(x, n2)]
    return [a + mm(b, q) for a, b, q in zip(x, m2, t)]


def direct_inverse_cholesky(s):
    i = lax.broadcasted_iota(jnp.int32, (K, K), 0)
    i2 = lax.broadcasted_iota(jnp.int32, (K, 2 * K), 0)
    j2 = lax.broadcasted_iota(jnp.int32, (K, 2 * K), 1)
    t0 = jnp.concatenate([s, (i == lax.broadcasted_iota(jnp.int32, (K, K), 1)).astype(jnp.float32)], axis=1)

    def step(j, t):
        row = jnp.sum(jnp.where(i2 == j, t, 0.0), axis=0, keepdims=True)
        col = jnp.sum(jnp.where(j2 == j, t, 0.0), axis=1, keepdims=True)
        piv = jnp.sum(jnp.where(j2[:1] == j, row, 0.0), axis=1, keepdims=True)
        new = row * lax.rsqrt(piv)
        t = t - jnp.where(i2 > j, col * lax.rsqrt(piv), 0.0) * new
        return jnp.where(i2 == j, new, t)

    return lax.fori_loop(0, K, step, t0)[:, K:]


def pair_factors(a_list, c_list, b_list, out_refs, flags, parts=None):
    eye, phi = grids()
    shifts = [jnp.sum(b * eye) / K for b in b_list]
    on = [f > 0 for f in flags]
    a_s = [jnp.where(f, a - s * eye, eye) for f, a, s in zip(on, a_list, shifts)]
    c_list = [jnp.where(f, c, 0.0) for f, c in zip(on, c_list)]
    nop = [jnp.where(f, b - s * eye, 0.0) for f, b, s in zip(on, b_list, shifts)]
    m, e0 = fast_inverse(a_s, eye)

    def rest(m, chol):
        x = finish(m, c_list, nop)
        xt = [v.T for v in x]
        grams = [eye + mm(v, v, NT) for v in xt] + [eye + mm(v, v, NT) for v in x]
        w, e1 = chol(grams)
        n = len(x)
        for p in range(n):
            w1, w2 = w[p], w[n + p]
            keep = on[p]
            out_refs[p][:K, :K] = jnp.where(keep, -mm(w1, xt[p]), eye)
            out_refs[p][:K, K:] = jnp.where(keep, w1, 0.0)
            out_refs[p][K:, :K] = jnp.where(keep, w2, 0.0)
            out_refs[p][K:, K:] = jnp.where(keep, mm(w2, x[p]), eye)
            if parts is not None:
                parts[p, 0] = jnp.where(keep, x[p], eye)
                parts[p, 1] = jnp.where(keep, w1, -eye)
                parts[p, 2] = jnp.where(keep, w2, eye)
        return e1

    e1 = rest(m, lambda g: fast_inverse_cholesky(g, eye, phi))
    good = jnp.logical_and(e0 < 1e-5, e1 < 6e-3)

    @pl.when(jnp.logical_not(good))
    def _():
        inv = []
        for a in a_s:
            at = a.T
            w = direct_inverse_cholesky(mm(at, at, NT))
            inv.append(mm(mm(w.T, w.T, NT), at))
        rest(inv, lambda g: ([direct_inverse_cholesky(v) for v in g], jnp.float32(0)))


def pick(odd, when_odd, when_even):
    return jnp.where(odd, when_odd, when_even)


def prepare_kernel(mask_ref, tile_ref, whole_ref, left_ref, own_ref):
    odd = lax.axis_index("row") % 2 == 1
    i = lax.broadcasted_iota(jnp.int32, (8, K), 0)
    j = lax.broadcasted_iota(jnp.int32, (8, K), 1)
    first = (mask_ref[0, 0] > 0).astype(jnp.float32)
    second = (mask_ref[1, 0] > 0).astype(jnp.float32)
    flags = jnp.where(j == 0, jnp.where(i == 7, first, jnp.where(i == 6, second, 0.0)), 0.0)
    whole_ref[...] = tile_ref[...]
    whole_ref[2 * K - 8 :, :K] = flags
    left_ref[...] = tile_ref[:, : 2 * K]
    own_ref[...] = pick(odd, tile_ref[:, 2 * K :], tile_ref[:, : 2 * K])
    own_ref[2 * K - 8 :, :K] = flags


def flags_of(ref):
    corner = ref[2 * K - 8 :, :K]
    i = lax.broadcasted_iota(jnp.int32, (8, K), 0)
    return jnp.sum(jnp.where(i == 7, corner, 0.0)) > 0.5, jnp.sum(jnp.where(i == 6, corner, 0.0)) > 0.5


def steps_kernel(mask_ref, tile_ref, partner_ref, above_ref, right_ref, next_ref, row_ref, col_ref, f1, f2, parts):
    row = lax.axis_index("row")
    col = lax.axis_index("col")
    odd = row % 2 == 1
    owner = col == row // 2

    @pl.when(jnp.logical_not(owner))
    def _():
        row_ref[...] = jnp.zeros_like(row_ref)
        col_ref[...] = jnp.zeros_like(col_ref)

    @pl.when(owner)
    def _():
        W = 2 * K
        d0 = lambda i, j: pick(odd, tile_ref[i, W + j.start : W + j.stop], tile_ref[i, j])
        dm = lambda i, j: pick(odd, partner_ref[i, j], next_ref[i, j])
        dp = lambda i, j: pick(odd, next_ref[i, j], partner_ref[i, W + j.start : W + j.stop])
        lo, hi = slice(0, K), slice(K, W)
        partner1, partner2 = flags_of(partner_ref)
        next1, next2 = flags_of(next_ref)
        odd_i = odd.astype(jnp.int32)
        p1, p2, n1, n2 = [v.astype(jnp.int32) for v in (partner1, partner2, next1, next2)]
        m_flag = odd_i * p1 + (1 - odd_i) * n1
        m_flag2 = odd_i * p2 + (1 - odd_i) * n2
        p_flag = odd_i * n1 + (1 - odd_i) * p1
        blocks = (dm, d0, dp)
        pair_factors(
            [d(lo, lo) for d in blocks],
            [d(lo, hi) for d in blocks],
            [d(hi, hi) for d in blocks],
            [f1.at[p] for p in range(3)],
            [m_flag, mask_ref[0, 0], p_flag],
            parts,
        )

        def congruent(f, d):
            left, right = f[:, :K], f[:, K:]
            g = jnp.concatenate([mm(left, d(lo, lo)), mm(left, d(lo, hi)) + mm(right, d(hi, hi))], axis=1)
            return mm(g, f, NT)

        am = pick(odd, partner_ref[:, W:], above_ref[...])
        a0 = pick(odd, right_ref[...], tile_ref[:, W:])
        fm_low, f0_top, f0_low, fp_top = f1[0, K:, :], f1[1, :K, :], f1[1, K:, :], f1[2, :K, :]
        pair_factors(
            [congruent(fm_low, dm), congruent(f0_low, d0)],
            [mm(mm(fm_low, am), f0_top, NT), mm(mm(f0_low, a0), fp_top, NT)],
            [congruent(f0_top, d0), congruent(fp_top, dp)],
            [f2.at[p] for p in range(2)],
            [m_flag2, mask_ref[1, 0]],
        )
        eye, phi = grids()
        low = phi > 0.25

        def packed(lower, second):
            return jnp.where(low, lower, second.T), jnp.sum(second * eye, axis=0, keepdims=True)

        fm_x, f0_x, fp_x = parts[0, 0], parts[1, 0], parts[2, 0]
        z2 = mm(f2[0, K:, K:], parts[1, 1])
        z3 = mm(f2[1, :K, :K], parts[1, 2])
        row_y, row_diag = packed(mm(f2[0, K:, :K], parts[0, 2]), mm(f2[1, :K, K:], parts[2, 1]))
        col_y, col_diag = packed(mm(f2[1, K:, :K], parts[1, 2]), mm(f2[0, :K, K:], parts[1, 1]))
        i = lax.broadcasted_iota(jnp.int32, (8, K), 0)
        am_, a0_, ap_ = [(f > 0).astype(jnp.float32) for f in (m_flag, mask_ref[0, 0], p_flag)]
        for out, values, diag, marks in (
            (row_ref, (fm_x, f0_x, fp_x, z2, z3, row_y), row_diag, (am_, a0_, ap_)),
            (col_ref, (f0_x, z2, z3, col_y), col_diag, (a0_,)),
        ):
            for n, value in enumerate(values):
                out[n * K : (n + 1) * K, :] = value
            tail = jnp.where(i == 0, diag, 0.0)
            for n, mark in enumerate(marks):
                tail = jnp.where(i == n + 1, mark, tail)
            out[len(values) * K :, :] = tail


def unpacked(both, tail):
    eye, phi = grids()
    low = phi > 0.25
    return jnp.where(low, both, 0.0), jnp.where(low, 0.0, both).T + eye * tail[0:1, :]


def rows_kernel(step_ref, up_ref, own_ref, down_ref, out_ref):
    xm, x0, xp, z2, z3, both = [step_ref[n * K : (n + 1) * K, :] for n in range(6)]
    tail = step_ref[6 * K :, :]
    y1, y4 = unpacked(both, tail)
    am, a0, ap = [tail[n : n + 1, :1] for n in (1, 2, 3)]
    x0t, xpt = x0.T, xp.T
    own_top, own_low = own_ref[:K, :], own_ref[K:, :]
    t1 = am * up_ref[:K, :] + mm(xm, up_ref[K:, :])
    t2 = a0 * own_low - mm(x0t, own_top)
    t3 = a0 * own_top + mm(x0, own_low)
    t4 = ap * down_ref[K:, :] - mm(xpt, down_ref[:K, :])
    out_ref[:K, :] = mm(y1, t1) + mm(z2, t2)
    out_ref[K:, :] = mm(z3, t3) + mm(y4, t4)


def col_parts(mine_ref, other_ref):
    odd = lax.axis_index("row") % 2 == 1
    mine, other = mine_ref[...], other_ref[...]
    for message in (pick(odd, other, mine), pick(odd, mine, other)):
        x, z2, z3, both = [message[n * K : (n + 1) * K, :] for n in range(4)]
        tail = message[4 * K :, :]
        y1, y4 = unpacked(both, tail)
        yield x, z2, z3, y1, y4, tail[1:2, :1]


def edges_kernel(mine_ref, other_ref, rows_ref, to_left_ref, to_right_ref):
    (xe, _, _, _, y4e, ae), (xo, _, _, y1o, _, ao) = col_parts(mine_ref, other_ref)
    le, re, lo, ro = [rows_ref[:, n * K : (n + 1) * K] for n in range(4)]
    to_left_ref[...] = mm(ae * re - mm(le, xe), y4e, NT)
    to_right_ref[...] = mm(ao * lo + mm(ro, xo, NT), y1o, NT)


def inner_kernel(mine_ref, other_ref, rows_ref, out_ref):
    (xe, z2e, z3e, y1e, _, ae), (xo, z2o, z3o, _, y4o, ao) = col_parts(mine_ref, other_ref)
    le, re, lo, ro = [rows_ref[:, n * K : (n + 1) * K] for n in range(4)]
    ue = ae * re - mm(le, xe)
    ve = ae * le + mm(re, xe, NT)
    uo = ao * ro - mm(lo, xo)
    vo = ao * lo + mm(ro, xo, NT)
    out_ref[:, :K] = mm(ue, z2e, NT)
    out_ref[:, K : 2 * K] = mm(ve, z3e, NT) + mm(uo, y4o, NT)
    out_ref[:, 2 * K : 3 * K] = mm(uo, z2o, NT) + mm(ve, y1e, NT)
    out_ref[:, 3 * K :] = mm(vo, z3o, NT)


def local(kernel, shapes, args, scratch=(), masks=0):
    smem = pl.BlockSpec(memory_space=pltpu.SMEM)
    vmem = pl.BlockSpec(memory_space=pltpu.VMEM)
    return pl.pallas_call(
        kernel,
        out_shape=[jax.ShapeDtypeStruct(shape, jnp.float32) for shape in shapes],
        in_specs=[smem] * masks + [vmem] * (len(args) - masks),
        out_specs=[vmem] * len(shapes),
        scratch_shapes=list(scratch),
    )(*args)


def trees(row_value, col_value, cols):
    at = lambda r, c: r * cols + c
    row_lists = [
        [at(r, c) for c in range(r // 2, cols)] + ([at(r, r // 2 - 1)] if r % 2 == 0 and r else [])
        for r in range(2 * cols)
    ]
    col_lists = [
        [at(2 * q + k, c) for q in range(c, -1, -1)] + ([at(2 * c + 2 + k, c)] if c + 1 < cols else [])
        for k in range(2)
        for c in range(cols)
    ]
    orders = ((8, 4, 2, 1), (1, 8, 4, 2))
    sources = [[0], [0]]

    def pairs(lists, core, i):
        step = orders[core][i]
        return [(line[s], line[s + step]) for line in lists for s in sources[core] if s + step < len(line)]

    for i in range(4):
        row_in = lax.ppermute(row_value, AXES, pairs(row_lists[::2], 0, i) + pairs(row_lists[1::2], 1, i))
        col_in = lax.ppermute(col_value, AXES, pairs(col_lists[:cols], 0, i) + pairs(col_lists[cols:], 1, i))
        row_value, col_value = lax.optimization_barrier((row_value + row_in, col_value + col_in))
        sources = [s + [v + orders[k][i] for v in s] for k, s in enumerate(sources)]
    swap = [(at(2 * q + k, c), at(2 * q + 1 - k, c)) for c in range(cols) for q in range(min(c + 2, cols)) for k in range(2)]
    return row_value, col_value, lax.ppermute(col_value, AXES, swap)


def body(tile, mask):
    rows = lax.axis_size("row")
    cols = lax.axis_size("col")
    at = lambda r, c: r * cols + c
    W = 2 * K
    send = lambda value, pairs: lax.ppermute(value, AXES, pairs)
    whole, left, own = local(prepare_kernel, [(W, 2 * W), (W, W), (W, W)], (mask, tile), masks=1)
    partner = send(whole, [(at(2 * c + k, c), at(2 * c + 1 - k, c)) for c in range(cols) for k in range(2)])
    above = send(left, [(at(2 * c - 1, c), at(2 * c, c)) for c in range(1, cols)])
    right = send(left, [(at(2 * c + 1, c + 1), at(2 * c + 1, c)) for c in range(cols - 1)])
    beside = send(
        own,
        [(at(2 * c - 1, c - 1), at(2 * c, c)) for c in range(1, cols)]
        + [(at(2 * c + 2, c + 1), at(2 * c + 1, c)) for c in range(cols - 1)],
    )
    tile_late, partner, above, right, beside = lax.optimization_barrier((tile, partner, above, right, beside))
    live = [(r, c) for r in range(rows) for c in range(r // 2, cols)]
    up = send(tile_late, [(at(r, c), at(r + 1, c)) for r, c in live if r + 1 < rows])
    down = send(tile_late, [(at(r, c), at(r - 1, c)) for r, c in live if r])
    row_step, col_step = local(
        steps_kernel,
        [(6 * K + 8, K), (4 * K + 8, K)],
        (mask, tile, partner, above, right, beside),
        scratch=(
            pltpu.VMEM((3, W, W), jnp.float32),
            pltpu.VMEM((2, W, W), jnp.float32),
            pltpu.VMEM((3, 3, K, K), jnp.float32),
        ),
        masks=1,
    )
    row_step, mine, other = trees(row_step, col_step, cols)
    done_rows = local(rows_kernel, [(W, 2 * W)], (row_step, up, tile, down))[0]
    to_left, to_right = local(edges_kernel, [(W, K), (W, K)], (mine, other, done_rows))
    full = [(r, c) for r in range(rows) for c in range(max((r - 1) // 2, 0), cols)]
    before = send(to_right, [(at(r, c), at(r, c + 1)) for r, c in full if c + 1 < cols])
    after = send(to_left, [(at(r, c), at(r, c - 1)) for r, c in full if c])
    inner = local(inner_kernel, [(W, 2 * W)], (mine, other, done_rows))[0]
    return jnp.concatenate([inner[:, :K] + before, inner[:, K : 3 * K], inner[:, 3 * K :] + after], axis=1)


def solution(mesh):
    placed = (P("row", "col"), P(None, "row"))
    return jax.shard_map(body, mesh=mesh, in_specs=placed, out_specs=P("row", "col"), check_vma=False)
```

profile of v0, /device:TPU:8, one launch (start us, length us, event | category | flops | bytes accessed | tf_op | source)
XLA Modules:
  0.0 366.2 jit_solution(8312088440078474498)
XLA Ops:
  0.0 1.3 copy.4.mask_ref
  1.3 2.0 shard_map.28
  3.3 0.7 collective-permute-start
  4.0 0.7 collective-permute-start.1
  4.7 0.7 collective-permute-start.2
  5.4 0.7 collective-permute-start.3
  6.1 0.0 collective-permute-done.1.above_ref
  6.1 0.0 copy-start.8
  6.1 0.0 collective-permute-done.2.right_ref
  6.1 0.0 copy-start.9
  6.1 0.0 collective-permute-done.3.next_ref
  6.1 0.0 copy-start.10
  6.1 0.0 collective-permute-done.partner_ref
  6.2 0.6 copy-done.8
  6.8 0.1 copy-done.9
  6.9 0.1 copy-done.10
  7.0 0.0 copy-start.4
  7.0 0.8 copy-done.4
  7.8 2.3 shard_map.29
  10.1 0.7 collective-permute-start.4
  10.8 0.0 copy-start.7
  10.8 0.8 collective-permute-start.5
  11.7 0.0 collective-permute-done.5
  11.7 1.0 add.31
  12.7 0.0 collective-permute-done.4
  12.7 0.0 copy-done.7
  12.7 0.1 add.30
  12.7 0.7 collective-permute-start.6
  13.4 0.7 collective-permute-start.7
  14.1 0.0 collective-permute-done.7
  14.2 0.0 collective-permute-done.6
  14.2 0.9 collective-permute-start.8
  15.1 0.7 collective-permute-start.9
  15.8 0.0 collective-permute-done.9
  15.8 0.0 copy-start
  15.9 0.0 collective-permute-done.8
  15.9 1.4 collective-permute-start.10
  17.4 1.3 collective-permute-start.11
  18.7 0.0 copy-done
  18.7 1.3 collective-permute-start.13
  20.0 0.7 collective-permute-start.14
  20.7 144.0 %collective-permute-done.11 = f32[520,128]{1,0:T(8,128)S(1)} collective-permute-done((f32[520,128]{1,0:T(8,128)S(1)}, f32[520,128]{1,0:T(8,128)S(1)}, u32[]{:S(2)}, u32[]{:S(2)}) %collective-permute-start.11) | collective-permute-done | bytes 266272 | tf_op jit(solution)/shard_map/ppermute | solution.py:329
  164.7 0.0 copy-start.1
  164.7 181.1 %collective-permute-done.10 = f32[776,128]{1,0:T(8,128)S(1)} collective-permute-done((f32[776,128]{1,0:T(8,128)S(1)}, f32[776,128]{1,0:T(8,128)S(1)}, u32[]{:S(2)}, u32[]{:S(2)}) %collective-permute-start.10) | collective-permute-done | bytes 397344 | tf_op jit(solution)/shard_map/ppermute | solution.py:328
  345.9 0.8 add.36.step_ref
  346.7 0.0 copy-done.1
  346.7 1.9 collective-permute-start.12
  348.6 0.0 collective-permute-done.13.up_ref
  348.6 0.0 copy-start.5
  348.6 0.0 collective-permute-done.14.down_ref
  348.6 0.8 copy-done.5
  349.4 0.8 copy-done.6
  350.2 3.3 shard_map.30.rows_ref
  353.5 0.0 collective-permute-done.12.other_ref
  353.5 0.7 copy-done.3
  354.2 2.4 shard_map.32
  356.6 1.3 collective-permute-start.15
  357.9 1.3 collective-permute-start.16
  359.2 2.7 shard_map.31
  361.9 0.0 collective-permute-done.15
  361.9 3.4 collective-permute-done.16
  365.3 0.0 copy-done.2
  365.3 0.0 slice-done
  365.4 0.9 pad_maximum_fusion
  (10 shorter events, 0.3 us)
Async XLA Ops:
  3.3 2.8 collective-permute-start
  4.0 2.1 collective-permute-start.1
  4.7 1.4 collective-permute-start.2
  5.4 0.7 collective-permute-start.3
  6.1 0.7 copy-start.8
  6.1 0.8 copy-start.9
  6.1 0.9 copy-start.10
  7.0 0.8 copy-start.4
  10.1 2.5 collective-permute-start.4
  10.8 1.8 copy-start.7
  10.8 0.8 collective-permute-start.5
  12.7 1.4 collective-permute-start.6
  13.4 0.7 collective-permute-start.7
  14.2 1.6 collective-permute-start.8
  15.1 0.7 collective-permute-start.9
  15.8 2.8 copy-start
  15.9 329.9 %collective-permute-start.10 = (f32[776,128]{1,0:T(8,128)S(1)}, f32[776,128]{1,0:T(8,128)S(1)}, u32[]{:S(2)}, u32[]{:S(2)}) collective-permute-start(f32[776,128]{1,0:T(8,128)S(1)} %add.34), channel_id=1, source_target_pairs={{0,1},{8,9},{4,5},{12,13},{2,3},{10,11},{6,7},{14,15},{33,34},{41,... | collective-permute-start | bytes 1191944 | tf_op jit(solution)/shard_map/ppermute | solution.py:328
  17.4 147.3 %collective-permute-start.11 = (f32[520,128]{1,0:T(8,128)S(1)}, f32[520,128]{1,0:T(8,128)S(1)}, u32[]{:S(2)}, u32[]{:S(2)}) collective-permute-start(f32[520,128]{1,0:T(8,128)S(1)} %add.35), channel_id=1, source_target_pairs={{0,32},{33,1},{66,34},{2,98},{99,67},{35,3},{132,100},{4,164},{68,... | collective-permute-start | bytes 798728 | tf_op jit(solution)/shard_map/ppermute | solution.py:329
  18.7 329.9 %collective-permute-start.13 = (f32[256,512]{1,0:T(8,128)S(1)}, f32[256,512]{1,0:T(8,128)S(1)}, u32[]{:S(2)}, u32[]{:S(2)}) collective-permute-start(f32[256,512]{1,0:T(8,128)S(1)} %copy-done), channel_id=1, source_target_pairs={{0,16},{1,17},{2,18},{3,19},{4,20},{5,21},{6,22},{7,23},{8,24},{9,... | collective-permute-start | bytes 1572872 | tf_op jit(solution)/shard_map/ppermute | solution.py:341
  20.0 328.7 %collective-permute-start.14 = (f32[256,512]{1,0:T(8,128)S(1)}, f32[256,512]{1,0:T(8,128)S(1)}, u32[]{:S(2)}, u32[]{:S(2)}) collective-permute-start(f32[256,512]{1,0:T(8,128)S(1)} %copy-done), channel_id=1, source_target_pairs={{16,0},{17,1},{18,2},{19,3},{20,4},{21,5},{22,6},{23,7},{24,8},{25... | collective-permute-start | bytes 1572872 | tf_op jit(solution)/shard_map/ppermute | solution.py:341
  164.7 182.0 %copy-start.1 = (f32[520,128]{1,0:T(8,128)}, f32[520,128]{1,0:T(8,128)S(1)}, u32[]{:S(2)}) copy-start(f32[520,128]{1,0:T(8,128)S(1)} %add.37.mine_ref) | copy-start | bytes 798724
  346.7 6.8 %collective-permute-start.12 = (f32[520,128]{1,0:T(8,128)S(1)}, f32[520,128]{1,0:T(8,128)S(1)}, u32[]{:S(2)}, u32[]{:S(2)}) collective-permute-start(f32[520,128]{1,0:T(8,128)S(1)} %add.37.mine_ref), channel_id=1, source_target_pairs={{0,16},{16,0},{32,48},{48,32},{1,17},{17,1},{33,49},{49,33},{65,81... | collective-permute-start | bytes 798728 | tf_op jit(solution)/shard_map/ppermute | solution.py:333
  348.6 0.8 copy-start.5
  349.4 0.8 copy-start.6
  353.5 0.7 copy-start.3
  356.6 5.3 %collective-permute-start.15 = (f32[256,128]{1,0:T(8,128)}, f32[256,128]{1,0:T(8,128)S(1)}, u32[]{:S(2)}, u32[]{:S(2)}) collective-permute-start(f32[256,128]{1,0:T(8,128)} %get-tuple-element.43), channel_id=1, source_target_pairs={{0,1},{1,2},{2,3},{3,4},{4,5},{5,6},{6,7},{7,8},{8,9},{9,10},{10,1... | collective-permute-start | bytes 393224 | tf_op jit(solution)/shard_map/ppermute | solution.py:341
  357.9 7.4 %collective-permute-start.16 = (f32[256,128]{1,0:T(8,128)}, f32[256,128]{1,0:T(8,128)S(1)}, u32[]{:S(2)}, u32[]{:S(2)}) collective-permute-start(f32[256,128]{1,0:T(8,128)} %get-tuple-element.44), channel_id=1, source_target_pairs={{1,0},{2,1},{3,2},{4,3},{5,4},{6,5},{7,6},{8,7},{9,8},{10,9},{11,1... | collective-permute-start | bytes 393224 | tf_op jit(solution)/shard_map/ppermute | solution.py:341
  361.9 3.4 copy-start.2
  361.9 3.4 slice-start
where the time goes:
time: 367 us; the launch traced here: 366 us
  waiting for transfers between devices  329 us (90%)
  starting transfers between devices  16.3 us (4%)
  Pallas kernels  12.8 us (3%)
  local copies, waits for them, and re-layouts  5.29 us (1%)
    ppermute x4, waiting for transfers between devices, trees(): lax.ppermute(row_value, AXES, pairs(row_lists[::2], 0, i) + pairs(row_lis...  181 us
    ppermute x4, waiting for transfers between devices, trees(): lax.ppermute(col_value, AXES, pairs(col_lists[:cols], 0, i) + pairs(col_l...  144 us
    pallas_call x5, Pallas kernels, local(): pl.pallas_call(kernel, out_shape=[jax.ShapeDtypeStruct(shape, jnp.float32...  12.8 us
  transfers between devices with their start and end apart: 17, of which 3 were waited for; matrix products, arithmetic and copies ran while one was open for 1% of the time, Pallas kernels for 2%

commit v1 on v0

--- a/solution.py
+++ b/solution.py
@@ -148,18 +148,15 @@
     return jnp.where(odd, when_odd, when_even)
 
 
-def prepare_kernel(mask_ref, tile_ref, whole_ref, left_ref, own_ref):
+def prepare_kernel(mask_ref, tile_ref, own_ref, coupling_ref):
     odd = lax.axis_index("row") % 2 == 1
     i = lax.broadcasted_iota(jnp.int32, (8, K), 0)
     j = lax.broadcasted_iota(jnp.int32, (8, K), 1)
-    first = (mask_ref[0, 0] > 0).astype(jnp.float32)
-    second = (mask_ref[1, 0] > 0).astype(jnp.float32)
-    flags = jnp.where(j == 0, jnp.where(i == 7, first, jnp.where(i == 6, second, 0.0)), 0.0)
-    whole_ref[...] = tile_ref[...]
-    whole_ref[2 * K - 8 :, :K] = flags
-    left_ref[...] = tile_ref[:, : 2 * K]
+    marks = (mask_ref[...] > 0).astype(jnp.float32)
+    flags = jnp.where(j == 0, jnp.where(i == 7, marks[0:1, :], jnp.where(i == 6, marks[1:2, :], 0.0)), 0.0)
     own_ref[...] = pick(odd, tile_ref[:, 2 * K :], tile_ref[:, : 2 * K])
     own_ref[2 * K - 8 :, :K] = flags
+    coupling_ref[...] = pick(odd, tile_ref[:, : 2 * K], tile_ref[:, 2 * K :])
 
 
 def flags_of(ref):
@@ -168,7 +165,7 @@
     return jnp.sum(jnp.where(i == 7, corner, 0.0)) > 0.5, jnp.sum(jnp.where(i == 6, corner, 0.0)) > 0.5
 
 
-def steps_kernel(mask_ref, tile_ref, partner_ref, above_ref, right_ref, next_ref, row_ref, col_ref, f1, f2, parts):
+def steps_kernel(own_ref, coupling_ref, partner_ref, beside_ref, near_ref, right_ref, row_ref, col_ref, f1, f2, parts):
     row = lax.axis_index("row")
     col = lax.axis_index("col")
     odd = row % 2 == 1
@@ -182,14 +179,14 @@
     @pl.when(owner)
     def _():
         W = 2 * K
-        d0 = lambda i, j: pick(odd, tile_ref[i, W + j.start : W + j.stop], tile_ref[i, j])
-        dm = lambda i, j: pick(odd, partner_ref[i, j], next_ref[i, j])
-        dp = lambda i, j: pick(odd, next_ref[i, j], partner_ref[i, W + j.start : W + j.stop])
+        d0 = lambda i, j: own_ref[i, j]
+        dm = lambda i, j: pick(odd, partner_ref[i, j], beside_ref[i, j])
+        dp = lambda i, j: pick(odd, beside_ref[i, j], partner_ref[i, j])
         lo, hi = slice(0, K), slice(K, W)
-        partner1, partner2 = flags_of(partner_ref)
-        next1, next2 = flags_of(next_ref)
         odd_i = odd.astype(jnp.int32)
-        p1, p2, n1, n2 = [v.astype(jnp.int32) for v in (partner1, partner2, next1, next2)]
+        own1, own2, p1, p2, n1, n2 = [
+            v.astype(jnp.int32) for ref in (own_ref, partner_ref, beside_ref) for v in flags_of(ref)
+        ]
         m_flag = odd_i * p1 + (1 - odd_i) * n1
         m_flag2 = odd_i * p2 + (1 - odd_i) * n2
         p_flag = odd_i * n1 + (1 - odd_i) * p1
@@ -199,7 +196,7 @@
             [d(lo, hi) for d in blocks],
             [d(hi, hi) for d in blocks],
             [f1.at[p] for p in range(3)],
-            [m_flag, mask_ref[0, 0], p_flag],
+            [m_flag, own1, p_flag],
             parts,
         )
 
@@ -208,15 +205,15 @@
             g = jnp.concatenate([mm(left, d(lo, lo)), mm(left, d(lo, hi)) + mm(right, d(hi, hi))], axis=1)
             return mm(g, f, NT)
 
-        am = pick(odd, partner_ref[:, W:], above_ref[...])
-        a0 = pick(odd, right_ref[...], tile_ref[:, W:])
+        am = near_ref[...]
+        a0 = pick(odd, right_ref[...], coupling_ref[...])
         fm_low, f0_top, f0_low, fp_top = f1[0, K:, :], f1[1, :K, :], f1[1, K:, :], f1[2, :K, :]
         pair_factors(
             [congruent(fm_low, dm), congruent(f0_low, d0)],
             [mm(mm(fm_low, am), f0_top, NT), mm(mm(f0_low, a0), fp_top, NT)],
             [congruent(f0_top, d0), congruent(fp_top, dp)],
             [f2.at[p] for p in range(2)],
-            [m_flag2, mask_ref[1, 0]],
+            [m_flag2, own2],
         )
         eye, phi = grids()
         low = phi > 0.25
@@ -230,7 +227,7 @@
         row_y, row_diag = packed(mm(f2[0, K:, :K], parts[0, 2]), mm(f2[1, :K, K:], parts[2, 1]))
         col_y, col_diag = packed(mm(f2[1, K:, :K], parts[1, 2]), mm(f2[0, :K, K:], parts[1, 1]))
         i = lax.broadcasted_iota(jnp.int32, (8, K), 0)
-        am_, a0_, ap_ = [(f > 0).astype(jnp.float32) for f in (m_flag, mask_ref[0, 0], p_flag)]
+        am_, a0_, ap_ = [(f > 0).astype(jnp.float32) for f in (m_flag, own1, p_flag)]
         for out, values, diag, marks in (
             (row_ref, (fm_x, f0_x, fp_x, z2, z3, row_y), row_diag, (am_, a0_, ap_)),
             (col_ref, (f0_x, z2, z3, col_y), col_diag, (a0_,)),
@@ -294,13 +291,12 @@
     out_ref[:, 3 * K :] = mm(vo, z3o, NT)
 
 
-def local(kernel, shapes, args, scratch=(), masks=0):
-    smem = pl.BlockSpec(memory_space=pltpu.SMEM)
+def local(kernel, shapes, args, scratch=()):
     vmem = pl.BlockSpec(memory_space=pltpu.VMEM)
     return pl.pallas_call(
         kernel,
         out_shape=[jax.ShapeDtypeStruct(shape, jnp.float32) for shape in shapes],
-        in_specs=[smem] * masks + [vmem] * (len(args) - masks),
+        in_specs=[vmem] * len(args),
         out_specs=[vmem] * len(shapes),
         scratch_shapes=list(scratch),
     )(*args)
@@ -317,6 +313,9 @@
         for k in range(2)
         for c in range(cols)
     ]
+    turned = lambda line: line[:1] + line[:0:-1]
+    row_lists[1::2] = [turned(line) for line in row_lists[1::2]]
+    col_lists[cols:] = [turned(line) for line in col_lists[cols:]]
     orders = ((8, 4, 2, 1), (1, 8, 4, 2))
     sources = [[0], [0]]
 
@@ -339,29 +338,31 @@
     at = lambda r, c: r * cols + c
     W = 2 * K
     send = lambda value, pairs: lax.ppermute(value, AXES, pairs)
-    whole, left, own = local(prepare_kernel, [(W, 2 * W), (W, W), (W, W)], (mask, tile), masks=1)
-    partner = send(whole, [(at(2 * c + k, c), at(2 * c + 1 - k, c)) for c in range(cols) for k in range(2)])
-    above = send(left, [(at(2 * c - 1, c), at(2 * c, c)) for c in range(1, cols)])
-    right = send(left, [(at(2 * c + 1, c + 1), at(2 * c + 1, c)) for c in range(cols - 1)])
+    own, coupling = local(prepare_kernel, [(W, W), (W, W)], (mask, tile))
+    partner = send(own, [(at(2 * c + k, c), at(2 * c + 1 - k, c)) for c in range(cols) for k in range(2)])
     beside = send(
         own,
         [(at(2 * c - 1, c - 1), at(2 * c, c)) for c in range(1, cols)]
         + [(at(2 * c + 2, c + 1), at(2 * c + 1, c)) for c in range(cols - 1)],
     )
-    tile_late, partner, above, right, beside = lax.optimization_barrier((tile, partner, above, right, beside))
+    near = send(
+        coupling,
+        [(at(2 * c, c), at(2 * c + 1, c)) for c in range(cols)]
+        + [(at(2 * c - 1, c), at(2 * c, c)) for c in range(1, cols)],
+    )
+    right = send(coupling, [(at(2 * c + 1, c + 1), at(2 * c + 1, c)) for c in range(cols - 1)])
     live = [(r, c) for r in range(rows) for c in range(r // 2, cols)]
-    up = send(tile_late, [(at(r, c), at(r + 1, c)) for r, c in live if r + 1 < rows])
-    down = send(tile_late, [(at(r, c), at(r - 1, c)) for r, c in live if r])
+    up = send(tile, [(at(r, c), at(r + 1, c)) for r, c in live if r + 1 < rows])
+    down = send(tile, [(at(r, c), at(r - 1, c)) for r, c in live if r])
     row_step, col_step = local(
         steps_kernel,
         [(6 * K + 8, K), (4 * K + 8, K)],
-        (mask, tile, partner, above, right, beside),
+        (own, coupling, partner, beside, near, right),
         scratch=(
             pltpu.VMEM((3, W, W), jnp.float32),
             pltpu.VMEM((2, W, W), jnp.float32),
             pltpu.VMEM((3, 3, K, K), jnp.float32),
         ),
-        masks=1,
     )
     row_step, mine, other = trees(row_step, col_step, cols)
     done_rows = local(rows_kernel, [(W, 2 * W)], (row_step, up, tile, down))[0]

time: 367 us -> 372 us (1.014)
  the two profiles are of different devices: /device:TPU:8 before, /device:TPU:19 now
where the time goes in v1:
time: 372 us; the launch traced here: 371 us
  waiting for transfers between devices  311 us (84%)
  starting transfers between devices  38.9 us (10%)
  Pallas kernels  12.5 us (3%)
  local copies, waits for them, and re-layouts  5.21 us (1%)
    ppermute x4, waiting for transfers between devices, trees(): lax.ppermute(col_value, AXES, pairs(col_lists[:cols], 0, i) + pairs(col_l...  190 us
    ppermute x8, waiting for transfers between devices, body(): send = lambda value, pairs: lax.ppermute(value, AXES, pairs)  121 us
    ppermute x1, starting transfers between devices, trees(): return (row_value, col_value, lax.ppermute(col_value, AXES, swap))  26.3 us
    pallas_call x5, Pallas kernels, local(): pl.pallas_call(kernel, out_shape=[jax.ShapeDtypeStruct(shape, jnp.float32...  12.5 us
  transfers between devices with their start and end apart: 17, of which 2 were waited for; matrix products, arithmetic and copies ran while one was open for 1% of the time, Pallas kernels for 2%

profile of v1, /device:TPU:19, one launch (start us, length us, event | category | flops | bytes accessed | tf_op | source)
XLA Modules:
  0.0 371.0 jit_solution(10549988621741903564)
XLA Ops:
  0.0 1.3 copy.3.mask_ref
  1.3 1.9 shard_map.28
  3.2 0.7 collective-permute-start
  3.9 0.7 collective-permute-start.1
  4.6 0.7 collective-permute-start.2
  5.3 0.7 collective-permute-start.3
  6.0 0.0 collective-permute-done.partner_ref
  6.0 0.0 copy-start.7
  6.0 0.0 collective-permute-done.1.beside_ref
  6.0 0.0 copy-start.8
  6.0 0.0 collective-permute-done.2.near_ref
  6.0 0.0 copy-start.9
  6.0 0.0 collective-permute-done.3.right_ref
  6.0 0.6 copy-done.7
  6.7 0.1 copy-done.8
  6.8 0.1 copy-done.9
  6.9 0.0 copy-start.10
  6.9 0.7 copy-done.10
  7.6 2.2 shard_map.29
  9.8 0.7 collective-permute-start.4
  10.5 0.0 copy-start.6
  10.5 1.4 collective-permute-start.5
  11.9 190.1 %collective-permute-done.5 = f32[520,128]{1,0:T(8,128)S(1)} collective-permute-done((f32[520,128]{1,0:T(8,128)}, f32[520,128]{1,0:T(8,128)S(1)}, u32[]{:S(2)}, u32[]{:S(2)}) %collective-permute-start.5) | collective-permute-done | bytes 266272 | tf_op jit(solution)/shard_map/ppermute | solution.py:328
  202.0 1.0 add.31
  203.0 0.0 collective-permute-done.4
  203.0 0.0 copy-done.6
  203.0 0.1 add.30
  203.1 0.7 collective-permute-start.6
  203.8 0.7 collective-permute-start.7
  204.5 0.0 collective-permute-done.7
  204.5 0.0 collective-permute-done.6
  204.6 0.9 collective-permute-start.8
  205.4 0.7 collective-permute-start.9
  206.1 0.0 collective-permute-done.9
  206.2 0.0 copy-start.2
  206.2 0.0 collective-permute-done.8
  206.3 0.8 collective-permute-start.10
  207.1 0.7 collective-permute-start.11
  207.8 0.0 copy-done.2
  207.8 0.7 collective-permute-start.13
  208.5 0.7 collective-permute-start.14
  209.2 0.0 collective-permute-done.11
  209.2 0.0 copy-start
  209.2 0.0 collective-permute-done.10
  209.3 0.8 add.36.step_ref
  210.1 0.0 copy-done
  210.1 26.3 %collective-permute-start.12 = (f32[520,128]{1,0:T(8,128)S(1)}, f32[520,128]{1,0:T(8,128)S(1)}, u32[]{:S(2)}, u32[]{:S(2)}) collective-permute-start(f32[520,128]{1,0:T(8,128)S(1)} %add.37.mine_ref), channel_id=1, source_target_pairs={{0,16},{16,0},{32,48},{48,32},{1,17},{17,1},{33,49},{49,33},{65,81... | collective-permute-start | bytes 798728 | tf_op jit(solution)/shard_map/ppermute | solution.py:332
  236.4 0.0 collective-permute-done.13.up_ref
  236.4 0.0 copy-start.4
  236.4 0.0 collective-permute-done.14.down_ref
  236.5 0.8 copy-done.4
  237.2 0.8 copy-done.5
  238.0 3.3 shard_map.30.rows_ref
  241.3 0.0 collective-permute-done.12.other_ref
  241.3 0.7 copy-done.3
  242.1 2.4 shard_map.32
  244.5 0.7 collective-permute-start.15
  245.1 1.3 collective-permute-start.16
  246.4 2.7 shard_map.31
  249.1 0.0 collective-permute-done.15
  249.1 121.0 %collective-permute-done.16 = f32[256,128]{1,0:T(8,128)S(1)} collective-permute-done((f32[256,128]{1,0:T(8,128)}, f32[256,128]{1,0:T(8,128)S(1)}, u32[]{:S(2)}, u32[]{:S(2)}) %collective-permute-start.16) | collective-permute-done | bytes 131104 | tf_op jit(solution)/shard_map/ppermute | solution.py:340
  370.1 0.0 copy-done.1
  370.2 0.0 slice-done
  370.2 0.9 pad_maximum_fusion
  (10 shorter events, 0.3 us)
Async XLA Ops:
  3.2 2.7 collective-permute-start
  3.9 2.1 collective-permute-start.1
  4.6 1.4 collective-permute-start.2
  5.3 0.7 collective-permute-start.3
  6.0 0.7 copy-start.7
  6.0 0.8 copy-start.8
  6.0 0.9 copy-start.9
  6.9 0.7 copy-start.10
  9.8 193.2 %collective-permute-start.4 = (f32[776,128]{1,0:T(8,128)}, f32[776,128]{1,0:T(8,128)S(1)}, u32[]{:S(2)}, u32[]{:S(2)}) collective-permute-start(f32[776,128]{1,0:T(8,128)} %get-tuple-element.21), channel_id=1, source_target_pairs={{0,8},{33,41},{66,74},{99,107},{132,140},{165,173},{198,206},{231,... | collective-permute-start | bytes 1191944 | tf_op jit(solution)/shard_map/ppermute | solution.py:327
  10.5 192.5 %copy-start.6 = (f32[776,128]{1,0:T(8,128)S(1)}, f32[776,128]{1,0:T(8,128)}, u32[]{:S(2)}) copy-start(f32[776,128]{1,0:T(8,128)} %get-tuple-element.21) | copy-start | bytes 1191940
  10.5 191.5 %collective-permute-start.5 = (f32[520,128]{1,0:T(8,128)}, f32[520,128]{1,0:T(8,128)S(1)}, u32[]{:S(2)}, u32[]{:S(2)}) collective-permute-start(f32[520,128]{1,0:T(8,128)} %get-tuple-element.22), channel_id=1, source_target_pairs={{231,263},{264,8},{297,41},{330,74},{363,107},{396,140},{429,173},... | collective-permute-start | bytes 798728 | tf_op jit(solution)/shard_map/ppermute | solution.py:328
  203.1 1.4 collective-permute-start.6
  203.8 0.7 collective-permute-start.7
  204.6 1.6 collective-permute-start.8
  205.4 0.7 collective-permute-start.9
  206.2 1.6 copy-start.2
  206.3 3.0 collective-permute-start.10
  207.1 2.1 collective-permute-start.11
  207.8 28.6 %collective-permute-start.13 = (f32[256,512]{1,0:T(8,128)S(1)}, f32[256,512]{1,0:T(8,128)S(1)}, u32[]{:S(2)}, u32[]{:S(2)}) collective-permute-start(f32[256,512]{1,0:T(8,128)S(1)} %copy-done.2), channel_id=1, source_target_pairs={{0,16},{1,17},{2,18},{3,19},{4,20},{5,21},{6,22},{7,23},{8,24},{9,... | collective-permute-start | bytes 1572872 | tf_op jit(solution)/shard_map/ppermute | solution.py:340
  208.5 28.0 %collective-permute-start.14 = (f32[256,512]{1,0:T(8,128)S(1)}, f32[256,512]{1,0:T(8,128)S(1)}, u32[]{:S(2)}, u32[]{:S(2)}) collective-permute-start(f32[256,512]{1,0:T(8,128)S(1)} %copy-done.2), channel_id=1, source_target_pairs={{16,0},{17,1},{18,2},{19,3},{20,4},{21,5},{22,6},{23,7},{24,8},{25... | collective-permute-start | bytes 1572872 | tf_op jit(solution)/shard_map/ppermute | solution.py:340
  209.2 0.8 copy-start
  210.1 31.3 %collective-permute-start.12 = (f32[520,128]{1,0:T(8,128)S(1)}, f32[520,128]{1,0:T(8,128)S(1)}, u32[]{:S(2)}, u32[]{:S(2)}) collective-permute-start(f32[520,128]{1,0:T(8,128)S(1)} %add.37.mine_ref), channel_id=1, source_target_pairs={{0,16},{16,0},{32,48},{48,32},{1,17},{17,1},{33,49},{49,33},{65,81... | collective-permute-start | bytes 798728 | tf_op jit(solution)/shard_map/ppermute | solution.py:332
  236.4 0.8 copy-start.4
  237.2 0.8 copy-start.5
  241.3 0.7 copy-start.3
  244.5 4.7 %collective-permute-start.15 = (f32[256,128]{1,0:T(8,128)}, f32[256,128]{1,0:T(8,128)S(1)}, u32[]{:S(2)}, u32[]{:S(2)}) collective-permute-start(f32[256,128]{1,0:T(8,128)} %get-tuple-element.31), channel_id=1, source_target_pairs={{0,1},{1,2},{2,3},{3,4},{4,5},{5,6},{6,7},{7,8},{8,9},{9,10},{10,1... | collective-permute-start | bytes 393224 | tf_op jit(solution)/shard_map/ppermute | solution.py:340
  245.1 125.0 %collective-permute-start.16 = (f32[256,128]{1,0:T(8,128)}, f32[256,128]{1,0:T(8,128)S(1)}, u32[]{:S(2)}, u32[]{:S(2)}) collective-permute-start(f32[256,128]{1,0:T(8,128)} %get-tuple-element.32), channel_id=1, source_target_pairs={{1,0},{2,1},{3,2},{4,3},{5,4},{6,5},{7,6},{8,7},{9,8},{10,9},{11,1... | collective-permute-start | bytes 393224 | tf_op jit(solution)/shard_map/ppermute | solution.py:340
  249.1 121.0 %copy-start.1 = (f32[256,512]{1,0:T(8,128)S(1)}, f32[256,512]{1,0:T(8,128)}, u32[]{:S(2)}) copy-start(f32[256,512]{1,0:T(8,128)} %shard_map.31) | copy-start | bytes 1572868
  249.1 121.0 %slice-start = ((f32[256,512]{1,0:T(8,128)}), f32[256,256]{1,0:T(8,128)S(1)}, s32[]{:S(2)}) async-start(f32[256,512]{1,0:T(8,128)} %shard_map.31), calls=%async_computation | async-start | bytes 524288 | tf_op jit(solution)/shard_map/slice | solution.py:374

commit v2 on v1

--- a/solution.py
+++ b/solution.py
@@ -153,7 +153,7 @@
     i = lax.broadcasted_iota(jnp.int32, (8, K), 0)
     j = lax.broadcasted_iota(jnp.int32, (8, K), 1)
     marks = (mask_ref[...] > 0).astype(jnp.float32)
-    flags = jnp.where(j == 0, jnp.where(i == 7, marks[0:1, :], jnp.where(i == 6, marks[1:2, :], 0.0)), 0.0)
+    flags = jnp.where(j == 0, jnp.where(i == 7, marks[:, 0:1], jnp.where(i == 6, marks[:, 1:2], 0.0)), 0.0)
     own_ref[...] = pick(odd, tile_ref[:, 2 * K :], tile_ref[:, : 2 * K])
     own_ref[2 * K - 8 :, :K] = flags
     coupling_ref[...] = pick(odd, tile_ref[:, : 2 * K], tile_ref[:, 2 * K :])
@@ -229,7 +229,7 @@
         i = lax.broadcasted_iota(jnp.int32, (8, K), 0)
         am_, a0_, ap_ = [(f > 0).astype(jnp.float32) for f in (m_flag, own1, p_flag)]
         for out, values, diag, marks in (
-            (row_ref, (fm_x, f0_x, fp_x, z2, z3, row_y), row_diag, (am_, a0_, ap_)),
+            (row_ref, (fm_x, f0_x, fp_x, z2, z3, row_y), row_diag, (a0_, am_, ap_)),
             (col_ref, (f0_x, z2, z3, col_y), col_diag, (a0_,)),
         ):
             for n, value in enumerate(values):
@@ -246,11 +246,23 @@
     return jnp.where(low, both, 0.0), jnp.where(low, 0.0, both).T + eye * tail[0:1, :]
 
 
-def rows_kernel(step_ref, up_ref, own_ref, down_ref, out_ref):
+def col_parts(mine_ref, other_ref):
+    odd = lax.axis_index("row") % 2 == 1
+    mine, other = mine_ref[...], other_ref[...]
+    for message in (pick(odd, other, mine), pick(odd, mine, other)):
+        x, z2, z3, both = [message[n * K : (n + 1) * K, :] for n in range(4)]
+        tail = message[4 * K :, :]
+        y1, y4 = unpacked(both, tail)
+        yield x, z2, z3, y1, y4, tail[1:2, :1]
+
+
+def rows_kernel(
+    step_ref, up_ref, own_ref, down_ref, mine_ref, other_ref, out_ref, to_left_ref, to_right_ref
+):
     xm, x0, xp, z2, z3, both = [step_ref[n * K : (n + 1) * K, :] for n in range(6)]
     tail = step_ref[6 * K :, :]
     y1, y4 = unpacked(both, tail)
-    am, a0, ap = [tail[n : n + 1, :1] for n in (1, 2, 3)]
+    a0, am, ap = [tail[n : n + 1, :1] for n in (1, 2, 3)]
     x0t, xpt = x0.T, xp.T
     own_top, own_low = own_ref[:K, :], own_ref[K:, :]
     t1 = am * up_ref[:K, :] + mm(xm, up_ref[K:, :])
@@ -259,21 +271,8 @@
     t4 = ap * down_ref[K:, :] - mm(xpt, down_ref[:K, :])
     out_ref[:K, :] = mm(y1, t1) + mm(z2, t2)
     out_ref[K:, :] = mm(z3, t3) + mm(y4, t4)
-
-
-def col_parts(mine_ref, other_ref):
-    odd = lax.axis_index("row") % 2 == 1
-    mine, other = mine_ref[...], other_ref[...]
-    for message in (pick(odd, other, mine), pick(odd, mine, other)):
-        x, z2, z3, both = [message[n * K : (n + 1) * K, :] for n in range(4)]
-        tail = message[4 * K :, :]
-        y1, y4 = unpacked(both, tail)
-        yield x, z2, z3, y1, y4, tail[1:2, :1]
-
-
-def edges_kernel(mine_ref, other_ref, rows_ref, to_left_ref, to_right_ref):
     (xe, _, _, _, y4e, ae), (xo, _, _, y1o, _, ao) = col_parts(mine_ref, other_ref)
-    le, re, lo, ro = [rows_ref[:, n * K : (n + 1) * K] for n in range(4)]
+    le, re, lo, ro = [out_ref[:, n * K : (n + 1) * K] for n in range(4)]
     to_left_ref[...] = mm(ae * re - mm(le, xe), y4e, NT)
     to_right_ref[...] = mm(ao * lo + mm(ro, xo, NT), y1o, NT)
 
@@ -316,7 +315,7 @@
     turned = lambda line: line[:1] + line[:0:-1]
     row_lists[1::2] = [turned(line) for line in row_lists[1::2]]
     col_lists[cols:] = [turned(line) for line in col_lists[cols:]]
-    orders = ((8, 4, 2, 1), (1, 8, 4, 2))
+    orders = ((8, 4, 2, 1), (2, 8, 4, 1))
     sources = [[0], [0]]
 
     def pairs(lists, core, i):
@@ -325,8 +324,9 @@
 
     for i in range(4):
         row_in = lax.ppermute(row_value, AXES, pairs(row_lists[::2], 0, i) + pairs(row_lists[1::2], 1, i))
+        row_value = lax.optimization_barrier(row_value + row_in)
         col_in = lax.ppermute(col_value, AXES, pairs(col_lists[:cols], 0, i) + pairs(col_lists[cols:], 1, i))
-        row_value, col_value = lax.optimization_barrier((row_value + row_in, col_value + col_in))
+        col_value = lax.optimization_barrier(col_value + col_in)
         sources = [s + [v + orders[k][i] for v in s] for k, s in enumerate(sources)]
     swap = [(at(2 * q + k, c), at(2 * q + 1 - k, c)) for c in range(cols) for q in range(min(c + 2, cols)) for k in range(2)]
     return row_value, col_value, lax.ppermute(col_value, AXES, swap)
@@ -338,7 +338,7 @@
     at = lambda r, c: r * cols + c
     W = 2 * K
     send = lambda value, pairs: lax.ppermute(value, AXES, pairs)
-    own, coupling = local(prepare_kernel, [(W, W), (W, W)], (mask, tile))
+    own, coupling = local(prepare_kernel, [(W, W), (W, W)], (mask.T, tile))
     partner = send(own, [(at(2 * c + k, c), at(2 * c + 1 - k, c)) for c in range(cols) for k in range(2)])
     beside = send(
         own,
@@ -365,9 +365,10 @@
         ),
     )
     row_step, mine, other = trees(row_step, col_step, cols)
-    done_rows = local(rows_kernel, [(W, 2 * W)], (row_step, up, tile, down))[0]
-    to_left, to_right = local(edges_kernel, [(W, K), (W, K)], (mine, other, done_rows))
     full = [(r, c) for r in range(rows) for c in range(max((r - 1) // 2, 0), cols)]
+    done_rows, to_left, to_right = local(
+        rows_kernel, [(W, 2 * W), (W, K), (W, K)], (row_step, up, tile, down, mine, other)
+    )
     before = send(to_right, [(at(r, c), at(r, c + 1)) for r, c in full if c + 1 < cols])
     after = send(to_left, [(at(r, c), at(r, c - 1)) for r, c in full if c])
     inner = local(inner_kernel, [(W, 2 * W)], (mine, other, done_rows))[0]

time: 372 us -> 365 us (0.981)
  the two profiles are of different devices: /device:TPU:19 before, /device:TPU:8 now
where the time goes in v2:
time: 365 us; the launch traced here: 364 us
  waiting for transfers between devices  262 us (72%)
  starting transfers between devices  84.6 us (23%)
  Pallas kernels  10.7 us (3%)
    ppermute x4, waiting for transfers between devices, trees(): lax.ppermute(col_value, AXES, pairs(col_lists[:cols], 0, i) + pairs(col_l...  141 us
    ppermute x4, waiting for transfers between devices, trees(): lax.ppermute(row_value, AXES, pairs(row_lists[::2], 0, i) + pairs(row_lis...  118 us
    ppermute x1, starting transfers between devices, trees(): return (row_value, col_value, lax.ppermute(col_value, AXES, swap))  70.2 us
    pallas_call x4, Pallas kernels, local(): pl.pallas_call(kernel, out_shape=[jax.ShapeDtypeStruct(shape, jnp.float32...  10.7 us
  transfers between devices with their start and end apart: 17, of which 4 were waited for; matrix products, arithmetic and copies ran while one was open for 1% of the time, Pallas kernels for 1%

profile of v2, /device:TPU:8, one launch (start us, length us, event | category | flops | bytes accessed | tf_op | source)
XLA Modules:
  0.0 364.3 jit_solution(12065525110946907290)
XLA Ops:
  0.0 1.9 shard_map.28
  1.9 0.7 collective-permute-start.1
  2.6 0.7 collective-permute-start
  3.3 0.7 collective-permute-start.3
  4.0 0.7 collective-permute-start.2
  4.6 0.0 collective-permute-done.1.beside_ref
  4.7 0.0 copy-start.7
  4.7 0.0 collective-permute-done.partner_ref
  4.7 0.0 copy-start.8
  4.7 0.0 collective-permute-done.3.right_ref
  4.7 0.0 copy-start.9
  4.7 0.0 collective-permute-done.2.near_ref
  4.7 0.6 copy-done.7
  5.4 0.1 copy-done.8
  5.5 0.1 copy-done.9
  5.6 0.0 copy-start.10
  5.6 0.7 copy-done.10
  6.3 2.2 shard_map.29
  8.5 0.7 collective-permute-start.9
  9.2 0.0 copy-start.6
  9.2 0.8 collective-permute-start.4
  10.0 0.0 collective-permute-done.9
  10.0 1.1 add.34
  11.1 0.7 collective-permute-start.10
  11.8 0.0 collective-permute-done.4
  11.8 0.0 copy-done.6
  11.9 0.7 collective-permute-start.5
  12.5 0.0 collective-permute-done.5
  12.6 0.9 collective-permute-start.6
  13.5 0.0 collective-permute-done.10
  13.5 0.0 copy-start.2
  13.5 0.8 collective-permute-start.11
  14.4 0.0 collective-permute-done.6
  14.4 1.3 collective-permute-start.7
  15.7 0.0 copy-done.2
  15.7 1.3 collective-permute-start.13
  17.0 0.7 collective-permute-start.14
  17.7 0.0 collective-permute-done.11
  17.8 1.3 collective-permute-start.12
  19.1 140.8 %collective-permute-done.7 = f32[520,128]{1,0:T(8,128)S(1)} collective-permute-done((f32[520,128]{1,0:T(8,128)S(1)}, f32[520,128]{1,0:T(8,128)S(1)}, u32[]{:S(2)}, u32[]{:S(2)}) %collective-permute-start.7) | collective-permute-done | bytes 266272 | tf_op jit(solution)/shard_map/ppermute | solution.py:328
  160.0 0.0 copy-start
  160.0 70.2 %collective-permute-start.8 = (f32[520,128]{1,0:T(8,128)S(1)}, f32[520,128]{1,0:T(8,128)S(1)}, u32[]{:S(2)}, u32[]{:S(2)}) collective-permute-start(f32[520,128]{1,0:T(8,128)S(1)} %add.33.mine_ref), channel_id=1, source_target_pairs={{0,16},{16,0},{32,48},{48,32},{1,17},{17,1},{33,49},{49,33},{65,81... | collective-permute-start | bytes 798728 | tf_op jit(solution)/shard_map/ppermute | solution.py:332
  230.2 118.5 %collective-permute-done.12 = f32[776,128]{1,0:T(8,128)S(1)} collective-permute-done((f32[776,128]{1,0:T(8,128)S(1)}, f32[776,128]{1,0:T(8,128)S(1)}, u32[]{:S(2)}, u32[]{:S(2)}) %collective-permute-start.12) | collective-permute-done | bytes 397344 | tf_op jit(solution)/shard_map/ppermute | solution.py:326
  348.7 0.8 add.37.step_ref
  349.5 0.0 copy-done
  349.5 0.0 collective-permute-done.13.up_ref
  349.5 0.0 copy-start.4
  349.5 0.0 collective-permute-done.14.down_ref
  349.5 0.0 copy-start.5
  349.5 0.0 collective-permute-done.8.other_ref
  349.5 0.8 copy-done.4
  350.3 0.2 copy-done.5
  350.5 0.0 copy-start.3
  350.5 0.7 copy-done.3
  351.2 3.8 %shard_map.30 = (f32[256,512]{1,0:T(8,128)}, f32[256,128]{1,0:T(8,128)}, f32[256,128]{1,0:T(8,128)}) custom-call(f32[776,128]{1,0:T(8,128)} %add.37.step_ref, f32[256,512]{1,0:T(8,128)} %copy-done.4, f32[256,512]{1,0:T(8,128)} %own_ref.1, f32[256,512]{1,0:T(8,128)} %copy-done.5, f32[520,128]{1,0:T(8,128)} %copy-done, f32[520,128]{1,0:T(8,128)} %copy-done.3), custom_call_target="tpu_custom_call" | custom-call | tf_op jit(solution)/shard_map/pallas_call | solution.py:295
  355.0 1.3 collective-permute-start.15
  356.3 1.3 collective-permute-start.16
  357.6 2.7 shard_map.31
  360.3 0.0 copy-start.1
  360.4 0.9 collective-permute-done.15
  361.3 2.1 collective-permute-done.16
  363.4 0.0 copy-done.1
  363.4 0.0 slice-done
  363.5 0.9 pad_maximum_fusion
  (8 shorter events, 0.3 us)
Async XLA Ops:
  1.9 2.7 collective-permute-start.1
  2.6 2.1 collective-permute-start
  3.3 1.4 collective-permute-start.3
  4.0 0.7 collective-permute-start.2
  4.7 0.7 copy-start.7
  4.7 0.8 copy-start.8
  4.7 0.9 copy-start.9
  5.6 0.7 copy-start.10
  8.5 1.5 collective-permute-start.9
  9.2 2.6 copy-start.6
  9.2 2.6 collective-permute-start.4
  11.1 2.4 collective-permute-start.10
  11.9 0.7 collective-permute-start.5
  12.6 1.8 collective-permute-start.6
  13.5 2.2 copy-start.2
  13.5 4.2 %collective-permute-start.11 = (f32[776,128]{1,0:T(8,128)S(1)}, f32[776,128]{1,0:T(8,128)S(1)}, u32[]{:S(2)}, u32[]{:S(2)}) collective-permute-start(f32[776,128]{1,0:T(8,128)S(1)} %add.35), channel_id=1, source_target_pairs={{0,2},{8,10},{4,6},{12,14},{33,35},{41,43},{37,39},{45,47},{66,68}... | collective-permute-start | bytes 1191944 | tf_op jit(solution)/shard_map/ppermute | solution.py:326
  14.4 145.5 %collective-permute-start.7 = (f32[520,128]{1,0:T(8,128)S(1)}, f32[520,128]{1,0:T(8,128)S(1)}, u32[]{:S(2)}, u32[]{:S(2)}) collective-permute-start(f32[520,128]{1,0:T(8,128)S(1)} %add.32), channel_id=1, source_target_pairs={{0,32},{33,1},{66,34},{2,98},{99,67},{35,3},{132,100},{4,164},{68,... | collective-permute-start | bytes 798728 | tf_op jit(solution)/shard_map/ppermute | solution.py:328
  15.7 333.8 %collective-permute-start.13 = (f32[256,512]{1,0:T(8,128)S(1)}, f32[256,512]{1,0:T(8,128)S(1)}, u32[]{:S(2)}, u32[]{:S(2)}) collective-permute-start(f32[256,512]{1,0:T(8,128)S(1)} %copy-done.2), channel_id=1, source_target_pairs={{0,16},{1,17},{2,18},{3,19},{4,20},{5,21},{6,22},{7,23},{8,24},{9,... | collective-permute-start | bytes 1572872 | tf_op jit(solution)/shard_map/ppermute | solution.py:340
  17.0 332.5 %collective-permute-start.14 = (f32[256,512]{1,0:T(8,128)S(1)}, f32[256,512]{1,0:T(8,128)S(1)}, u32[]{:S(2)}, u32[]{:S(2)}) collective-permute-start(f32[256,512]{1,0:T(8,128)S(1)} %copy-done.2), channel_id=1, source_target_pairs={{16,0},{17,1},{18,2},{19,3},{20,4},{21,5},{22,6},{23,7},{24,8},{25... | collective-permute-start | bytes 1572872 | tf_op jit(solution)/shard_map/ppermute | solution.py:340
  17.8 330.9 %collective-permute-start.12 = (f32[776,128]{1,0:T(8,128)S(1)}, f32[776,128]{1,0:T(8,128)S(1)}, u32[]{:S(2)}, u32[]{:S(2)}) collective-permute-start(f32[776,128]{1,0:T(8,128)S(1)} %add.36), channel_id=1, source_target_pairs={{0,1},{8,9},{4,5},{12,13},{2,3},{10,11},{6,7},{14,15},{33,34},{41,... | collective-permute-start | bytes 1191944 | tf_op jit(solution)/shard_map/ppermute | solution.py:326
  160.0 189.5 %copy-start = (f32[520,128]{1,0:T(8,128)}, f32[520,128]{1,0:T(8,128)S(1)}, u32[]{:S(2)}) copy-start(f32[520,128]{1,0:T(8,128)S(1)} %add.33.mine_ref) | copy-start | bytes 798724
  160.0 189.6 %collective-permute-start.8 = (f32[520,128]{1,0:T(8,128)S(1)}, f32[520,128]{1,0:T(8,128)S(1)}, u32[]{:S(2)}, u32[]{:S(2)}) collective-permute-start(f32[520,128]{1,0:T(8,128)S(1)} %add.33.mine_ref), channel_id=1, source_target_pairs={{0,16},{16,0},{32,48},{48,32},{1,17},{17,1},{33,49},{49,33},{65,81... | collective-permute-start | bytes 798728 | tf_op jit(solution)/shard_map/ppermute | solution.py:332
  349.5 0.8 copy-start.4
  349.5 1.0 copy-start.5
  350.5 0.7 copy-start.3
  355.0 6.2 %collective-permute-start.15 = (f32[256,128]{1,0:T(8,128)}, f32[256,128]{1,0:T(8,128)S(1)}, u32[]{:S(2)}, u32[]{:S(2)}) collective-permute-start(f32[256,128]{1,0:T(8,128)} %get-tuple-element.17), channel_id=1, source_target_pairs={{0,1},{1,2},{2,3},{3,4},{4,5},{5,6},{6,7},{7,8},{8,9},{9,10},{10,1... | collective-permute-start | bytes 393224 | tf_op jit(solution)/shard_map/ppermute | solution.py:340
  356.3 7.1 %collective-permute-start.16 = (f32[256,128]{1,0:T(8,128)}, f32[256,128]{1,0:T(8,128)S(1)}, u32[]{:S(2)}, u32[]{:S(2)}) collective-permute-start(f32[256,128]{1,0:T(8,128)} %get-tuple-element.18), channel_id=1, source_target_pairs={{1,0},{2,1},{3,2},{4,3},{5,4},{6,5},{7,6},{8,7},{9,8},{10,9},{11,1... | collective-permute-start | bytes 393224 | tf_op jit(solution)/shard_map/ppermute | solution.py:340
  360.3 3.1 copy-start.1
  360.3 3.1 slice-start

commit v3 on v2

--- a/solution.py
+++ b/solution.py
@@ -275,6 +275,11 @@
     le, re, lo, ro = [out_ref[:, n * K : (n + 1) * K] for n in range(4)]
     to_left_ref[...] = mm(ae * re - mm(le, xe), y4e, NT)
     to_right_ref[...] = mm(ao * lo + mm(ro, xo, NT), y1o, NT)
+
+
+def add_edges_kernel(inner_ref, before_ref, after_ref, out_ref):
+    first = pl.program_id(0) == 0
+    out_ref[...] = inner_ref[...] + jnp.where(first, before_ref[...], after_ref[...])
 
 
 def inner_kernel(mine_ref, other_ref, rows_ref, out_ref):
@@ -372,7 +377,17 @@
     before = send(to_right, [(at(r, c), at(r, c + 1)) for r, c in full if c + 1 < cols])
     after = send(to_left, [(at(r, c), at(r, c - 1)) for r, c in full if c])
     inner = local(inner_kernel, [(W, 2 * W)], (mine, other, done_rows))[0]
-    return jnp.concatenate([inner[:, :K] + before, inner[:, K : 3 * K], inner[:, 3 * K :] + after], axis=1)
+    whole_edge = pl.BlockSpec((W, K), lambda i: (0, 0))
+    edge = pl.BlockSpec((W, K), lambda i: (0, 3 * i))
+    return pl.pallas_call(
+        add_edges_kernel,
+        grid=(2,),
+        out_shape=jax.ShapeDtypeStruct((W, 2 * W), jnp.float32),
+        in_specs=[edge, whole_edge, whole_edge],
+        out_specs=edge,
+        input_output_aliases={0: 0},
+        name="add_edges",
+    )(inner, before, after)
 
 
 def solution(mesh):

time: 365 us -> 366 us (level)
  no operation moved by 1% of the time
where the time goes in v3:
time: 366 us
  waiting for transfers between devices  262 us (72%)
  starting transfers between devices  84.6 us (23%)
  Pallas kernels  12.4 us (3%)
  local copies, waits for them, and re-layouts  3.95 us (1%)
    ppermute x4, waiting for transfers between devices, trees(): lax.ppermute(col_value, AXES, pairs(col_lists[:cols], 0, i) + pairs(col_l...  141 us
    ppermute x4, waiting for transfers between devices, trees(): lax.ppermute(row_value, AXES, pairs(row_lists[::2], 0, i) + pairs(row_lis...  118 us
    ppermute x1, starting transfers between devices, trees(): return (row_value, col_value, lax.ppermute(col_value, AXES, swap))  70.3 us
    pallas_call x4, Pallas kernels, local(): pl.pallas_call(kernel, out_shape=[jax.ShapeDtypeStruct(shape, jnp.float32...  10.7 us
  transfers between devices with their start and end apart: 17, of which 4 were waited for; matrix products, arithmetic and copies ran while one was open for 1% of the time, Pallas kernels for 1%

profile of v3, /device:TPU:8, one launch (start us, length us, event | category | flops | bytes accessed | tf_op | source)
XLA Modules:
  0.0 365.8 jit_solution(11599839296761263902)
XLA Ops:
  0.0 1.9 shard_map.28
  1.9 0.7 collective-permute-start.1
  2.6 0.7 collective-permute-start
  3.3 0.7 collective-permute-start.3
  4.0 0.7 collective-permute-start.2
  4.6 0.0 collective-permute-done.1.beside_ref
  4.7 0.0 copy-start.6
  4.7 0.0 collective-permute-done.partner_ref
  4.7 0.0 copy-start.7
  4.7 0.0 collective-permute-done.3.right_ref
  4.7 0.0 copy-start.8
  4.7 0.0 collective-permute-done.2.near_ref
  4.7 0.6 copy-done.6
  5.4 0.1 copy-done.7
  5.5 0.1 copy-done.8
  5.6 0.0 copy-start.9
  5.6 0.7 copy-done.9
  6.3 2.2 shard_map.29
  8.6 0.7 collective-permute-start.9
  9.2 0.0 copy-start.5
  9.3 0.8 collective-permute-start.4
  10.1 0.0 collective-permute-done.9
  10.1 1.1 add.28
  11.1 0.7 collective-permute-start.10
  11.8 0.0 collective-permute-done.4
  11.8 0.0 copy-done.5
  11.9 0.7 collective-permute-start.5
  12.6 0.0 collective-permute-done.5
  12.6 0.9 collective-permute-start.6
  13.5 0.0 collective-permute-done.10
  13.6 0.0 copy-start.1
  13.6 0.8 collective-permute-start.11
  14.4 0.0 collective-permute-done.6
  14.4 1.3 collective-permute-start.7
  15.7 0.0 copy-done.1
  15.8 1.3 collective-permute-start.13
  17.1 0.7 collective-permute-start.14
  17.8 0.0 collective-permute-done.11
  17.8 1.3 collective-permute-start.12
  19.1 140.8 %collective-permute-done.7 = f32[520,128]{1,0:T(8,128)S(1)} collective-permute-done((f32[520,128]{1,0:T(8,128)S(1)}, f32[520,128]{1,0:T(8,128)S(1)}, u32[]{:S(2)}, u32[]{:S(2)}) %collective-permute-start.7) | collective-permute-done | bytes 266272 | tf_op jit(solution)/shard_map/ppermute | solution.py:333
  160.0 0.0 copy-start
  160.0 70.3 %collective-permute-start.8 = (f32[520,128]{1,0:T(8,128)S(1)}, f32[520,128]{1,0:T(8,128)S(1)}, u32[]{:S(2)}, u32[]{:S(2)}) collective-permute-start(f32[520,128]{1,0:T(8,128)S(1)} %add.27.mine_ref), channel_id=1, source_target_pairs={{0,16},{16,0},{32,48},{48,32},{1,17},{17,1},{33,49},{49,33},{65,81... | collective-permute-start | bytes 798728 | tf_op jit(solution)/shard_map/ppermute | solution.py:337
  230.3 118.5 %collective-permute-done.12 = f32[776,128]{1,0:T(8,128)S(1)} collective-permute-done((f32[776,128]{1,0:T(8,128)S(1)}, f32[776,128]{1,0:T(8,128)S(1)}, u32[]{:S(2)}, u32[]{:S(2)}) %collective-permute-start.12) | collective-permute-done | bytes 397344 | tf_op jit(solution)/shard_map/ppermute | solution.py:331
  348.7 0.8 add.31.step_ref
  349.5 0.0 copy-done
  349.5 0.0 collective-permute-done.13.up_ref
  349.5 0.0 copy-start.3
  349.5 0.0 collective-permute-done.14.down_ref
  349.6 0.0 copy-start.4
  349.6 0.0 collective-permute-done.8.other_ref
  349.6 0.8 copy-done.3
  350.3 0.2 copy-done.4
  350.5 0.0 copy-start.2
  350.5 0.7 copy-done.2
  351.2 3.8 %shard_map.30 = (f32[256,512]{1,0:T(8,128)}, f32[256,128]{1,0:T(8,128)}, f32[256,128]{1,0:T(8,128)}) custom-call(f32[776,128]{1,0:T(8,128)} %add.31.step_ref, f32[256,512]{1,0:T(8,128)} %copy-done.3, f32[256,512]{1,0:T(8,128)} %own_ref.1, f32[256,512]{1,0:T(8,128)} %copy-done.4, f32[520,128]{1,0:T(8,128)} %copy-done, f32[520,128]{1,0:T(8,128)} %copy-done.2), custom_call_target="tpu_custom_call" | custom-call | tf_op jit(solution)/shard_map/pallas_call | solution.py:300
  355.1 1.3 collective-permute-start.15
  356.3 1.3 collective-permute-start.16
  357.6 2.7 shard_map.31.inner_ref
  360.4 0.9 collective-permute-done.15.before_ref
  361.3 0.0 copy-start.10
  361.3 2.1 collective-permute-done.16.after_ref
  363.4 0.0 copy-done.10
  363.4 0.6 copy-done.11
  364.1 1.8 add_edges.1
  (7 shorter events, 0.2 us)
Async XLA Ops:
  1.9 2.7 collective-permute-start.1
  2.6 2.1 collective-permute-start
  3.3 1.4 collective-permute-start.3
  4.0 0.7 collective-permute-start.2
  4.7 0.7 copy-start.6
  4.7 0.8 copy-start.7
  4.7 0.9 copy-start.8
  5.6 0.7 copy-start.9
  8.6 1.5 collective-permute-start.9
  9.2 2.6 copy-start.5
  9.3 2.6 collective-permute-start.4
  11.1 2.4 collective-permute-start.10
  11.9 0.7 collective-permute-start.5
  12.6 1.8 collective-permute-start.6
  13.6 2.2 copy-start.1
  13.6 4.2 %collective-permute-start.11 = (f32[776,128]{1,0:T(8,128)S(1)}, f32[776,128]{1,0:T(8,128)S(1)}, u32[]{:S(2)}, u32[]{:S(2)}) collective-permute-start(f32[776,128]{1,0:T(8,128)S(1)} %add.29), channel_id=1, source_target_pairs={{0,2},{8,10},{4,6},{12,14},{33,35},{41,43},{37,39},{45,47},{66,68}... | collective-permute-start | bytes 1191944 | tf_op jit(solution)/shard_map/ppermute | solution.py:331
  14.4 145.5 %collective-permute-start.7 = (f32[520,128]{1,0:T(8,128)S(1)}, f32[520,128]{1,0:T(8,128)S(1)}, u32[]{:S(2)}, u32[]{:S(2)}) collective-permute-start(f32[520,128]{1,0:T(8,128)S(1)} %add.26), channel_id=1, source_target_pairs={{0,32},{33,1},{66,34},{2,98},{99,67},{35,3},{132,100},{4,164},{68,... | collective-permute-start | bytes 798728 | tf_op jit(solution)/shard_map/ppermute | solution.py:333
  15.8 333.8 %collective-permute-start.13 = (f32[256,512]{1,0:T(8,128)S(1)}, f32[256,512]{1,0:T(8,128)S(1)}, u32[]{:S(2)}, u32[]{:S(2)}) collective-permute-start(f32[256,512]{1,0:T(8,128)S(1)} %copy-done.1), channel_id=1, source_target_pairs={{0,16},{1,17},{2,18},{3,19},{4,20},{5,21},{6,22},{7,23},{8,24},{9,... | collective-permute-start | bytes 1572872 | tf_op jit(solution)/shard_map/ppermute | solution.py:345
  17.1 332.5 %collective-permute-start.14 = (f32[256,512]{1,0:T(8,128)S(1)}, f32[256,512]{1,0:T(8,128)S(1)}, u32[]{:S(2)}, u32[]{:S(2)}) collective-permute-start(f32[256,512]{1,0:T(8,128)S(1)} %copy-done.1), channel_id=1, source_target_pairs={{16,0},{17,1},{18,2},{19,3},{20,4},{21,5},{22,6},{23,7},{24,8},{25... | collective-permute-start | bytes 1572872 | tf_op jit(solution)/shard_map/ppermute | solution.py:345
  17.8 330.9 %collective-permute-start.12 = (f32[776,128]{1,0:T(8,128)S(1)}, f32[776,128]{1,0:T(8,128)S(1)}, u32[]{:S(2)}, u32[]{:S(2)}) collective-permute-start(f32[776,128]{1,0:T(8,128)S(1)} %add.30), channel_id=1, source_target_pairs={{0,1},{8,9},{4,5},{12,13},{2,3},{10,11},{6,7},{14,15},{33,34},{41,... | collective-permute-start | bytes 1191944 | tf_op jit(solution)/shard_map/ppermute | solution.py:331
  160.0 189.6 %copy-start = (f32[520,128]{1,0:T(8,128)}, f32[520,128]{1,0:T(8,128)S(1)}, u32[]{:S(2)}) copy-start(f32[520,128]{1,0:T(8,128)S(1)} %add.27.mine_ref) | copy-start | bytes 798724
  160.0 189.6 %collective-permute-start.8 = (f32[520,128]{1,0:T(8,128)S(1)}, f32[520,128]{1,0:T(8,128)S(1)}, u32[]{:S(2)}, u32[]{:S(2)}) collective-permute-start(f32[520,128]{1,0:T(8,128)S(1)} %add.27.mine_ref), channel_id=1, source_target_pairs={{0,16},{16,0},{32,48},{48,32},{1,17},{17,1},{33,49},{49,33},{65,81... | collective-permute-start | bytes 798728 | tf_op jit(solution)/shard_map/ppermute | solution.py:337
  349.5 0.8 copy-start.3
  349.6 1.0 copy-start.4
  350.5 0.7 copy-start.2
  355.1 6.2 %collective-permute-start.15 = (f32[256,128]{1,0:T(8,128)}, f32[256,128]{1,0:T(8,128)S(1)}, u32[]{:S(2)}, u32[]{:S(2)}) collective-permute-start(f32[256,128]{1,0:T(8,128)} %get-tuple-element.17), channel_id=1, source_target_pairs={{0,1},{1,2},{2,3},{3,4},{4,5},{5,6},{6,7},{7,8},{8,9},{9,10},{10,1... | collective-permute-start | bytes 393224 | tf_op jit(solution)/shard_map/ppermute | solution.py:345
  356.3 7.1 %collective-permute-start.16 = (f32[256,128]{1,0:T(8,128)}, f32[256,128]{1,0:T(8,128)S(1)}, u32[]{:S(2)}, u32[]{:S(2)}) collective-permute-start(f32[256,128]{1,0:T(8,128)} %get-tuple-element.18), channel_id=1, source_target_pairs={{1,0},{2,1},{3,2},{4,3},{5,4},{6,5},{7,6},{8,7},{9,8},{10,9},{11,1... | collective-permute-start | bytes 393224 | tf_op jit(solution)/shard_map/ppermute | solution.py:345
  361.3 2.1 copy-start.10
  363.4 0.6 copy-start.11
